TPU v7x, 32 devices: a whole 2x2x4 slice. The times are simulated.
32 devices in a mesh: dp: 4 (over z), row: 4 (over y, core), col: 2 (over x).
Axes of the slice: x: 2, y: 2, z: 4, core: 2. Of those that a mesh axis runs over, the one named last changes fastest.
Arguments:
- tokens: bfloat16 [8192, 2048], P(('dp', 'col'), 'row'), may hold values from -6 to 6
- seq_ids: int32 [8192], P('dp'), may hold values from 0 to 7, as said below
- block_ids: int32 [8192], P('dp'), may hold values from 0 to 5, as said below
- positions: int32 [8192], P('dp'), may hold values from 0 to 1535, as said below
- norm1_gain: float32 [2048], P('row'), may hold values from 0.5 to 1.5
- norm2_gain: float32 [2048], P('row'), may hold values from 0.5 to 1.5
- w_query: bfloat16 [2048, 2048], P('row', 'col'), may hold values from -0.1875 to 0.1875
- w_kv: bfloat16 [2048, 256], P('row'), may hold values from -0.1875 to 0.1875
- w_out: bfloat16 [2048, 2048], P('col', 'row'), may hold values from -2 to 2
- w_gate: bfloat16 [2048, 5632], P('row', 'col'), may hold values from -0.125 to 0.125
- w_up: bfloat16 [2048, 5632], P('row', 'col'), may hold values from -0.125 to 0.125
- w_down: bfloat16 [5632, 2048], P('col', 'row'), may hold values from -0.078125 to 0.078125
- grad_output: float32 [8192, 2048], P(('dp', 'col'), 'row'), may hold values from -6 to 6
Outputs:
- output: float32 [8192, 2048], P(('dp', 'col'), 'row')
- input_grad: float32 [8192, 2048], P(('dp', 'col'), 'row')
- grad_query: float32 [4, 512, 2048], P('row', 'dp', 'col')
- grad_kv: float32 [4, 512, 256], P('row', ('dp', 'col'))
- grad_out: float32 [2, 1024, 2048], P('col', 'dp', 'row')
- grad_gate: float32 [4, 512, 5632], P('row', 'dp', 'col')
- grad_up: float32 [4, 512, 5632], P('row', 'dp', 'col')
- grad_down: float32 [2, 2816, 2048], P('col', 'dp', 'row')
- grad_norm1: float32 [4, 512], P('row', ('dp', 'col'))
- grad_norm2: float32 [4, 512], P('row', ('dp', 'col'))
Inputs may be any that keep to these rules, and one draw needn't show every extreme that they name: `seq_ids`: tokens of one sequence lie in one aligned run of 2048 tokens; each run holds two sequences of whole 256-token blocks, each a quarter of the run or more; in the first run the first sequence has exactly 2 blocks. block_ids equal positions // 256. positions count from 0 at each sequence's first token.
All inputs are finite; a program needn't handle non-finite values.
Results may differ from a plain program's by a relative error of at most 0.023.
Values may be sent and summed in bfloat16 or wider, within the bound.
No kernel may reach another device: no remote copies, remote signals or barrier semaphores. Data moves between devices by JAX's collectives and lax.ppermute only.
A program may use at most 256 MiB of HBM per device.

v0:
```python
import jax
import jax.numpy as jnp
from jax import lax
from jax.sharding import PartitionSpec as P

D = 2048
EPS = 1e-05
ROPE_BASE = 500000.0
MASKED = -1e30
CONTRACT_ROWS = (((0,), (0,)), ((), ()))
CONTRACT_LAST = (((1,), (1,)), ((), ()))


def rope_tables(positions, head_width):
    halfway = head_width // 2
    frequency = ROPE_BASE ** (-2.0 * jnp.arange(halfway, dtype=jnp.float32) / head_width)
    angles = positions.astype(jnp.float32)[:, None] * frequency[None, :]
    return (jnp.cos(angles), jnp.sin(angles))


def rotate(operand, cosine, sine_part):
    halfway = operand.shape[-1] // 2
    first_half = operand[..., :halfway]
    second_half = operand[..., halfway:]
    return jnp.concatenate(
        [
            first_half * cosine - second_half * sine_part,
            second_half * cosine + first_half * sine_part,
        ],
        axis=-1,
    )


def rotate_back(operand, cosine, sine_part):
    halfway = operand.shape[-1] // 2
    first_half = operand[..., :halfway]
    second_half = operand[..., halfway:]
    return jnp.concatenate(
        [
            first_half * cosine + second_half * sine_part,
            second_half * cosine - first_half * sine_part,
        ],
        axis=-1,
    )


def row_total(operand):
    return lax.psum(operand, "row")


def gather_columns(operand):
    return lax.all_gather(operand, "col", axis=0, tiled=True)


def spread_columns(operand):
    return lax.psum_scatter(
        operand.astype(jnp.bfloat16), "col", scatter_dimension=0, tiled=True
    ).astype(jnp.float32)


def spread_rows(gathered, matrix, contract_dim):
    return lax.psum_scatter(
        lax.dot_general(
            gathered,
            matrix,
            (((1,), (contract_dim,)), ((), ())),
            preferred_element_type=jnp.float32,
        ),
        "row",
        scatter_dimension=0,
        tiled=True,
    )


def fold_rows(operand, matrix, contract_dim, partner, keeping):
    full_rows = operand.shape[0] * lax.axis_size("row")
    grad_shape = (partner.shape[1], operand.shape[1]) if partner is not None else (1, 1)
    grad_zero = jnp.zeros(grad_shape, jnp.float32)
    kept_zero = jnp.zeros((full_rows, operand.shape[1]) if keeping else (1, 1), operand.dtype)
    shard_rows = lax.all_gather(operand, "row", axis=0, tiled=True)
    grad_acc = grad_zero
    kept_rows = kept_zero
    row_block = lax.dot_general(
        shard_rows, matrix, (((1,), (contract_dim,)), ((), ())), preferred_element_type=jnp.float32
    )
    if partner is not None:
        grad_acc = lax.dot_general(
            partner, shard_rows, CONTRACT_ROWS, preferred_element_type=jnp.float32
        )
    if keeping:
        kept_rows = shard_rows
    return (row_block, grad_acc, kept_rows)


def norm_forward(residual, gain):
    rms_factor = lax.rsqrt(row_total(jnp.sum(residual * residual, axis=1)) / D + EPS)[:, None]
    return (rms_factor, (residual * rms_factor * gain[None, :]).astype(jnp.bfloat16))


def norm_backward(residual, rms_factor, gain, normed_grad):
    weighted = normed_grad * gain[None, :]
    inner_sum = row_total(jnp.sum(weighted * residual, axis=1))[:, None]
    input_part = (
        rms_factor * weighted - residual * (rms_factor * rms_factor * rms_factor) * inner_sum / D
    )
    return (input_part, jnp.sum(normed_grad * residual * rms_factor, axis=0))


def per_device(
    tokens,
    seq_ids,
    block_ids,
    positions,
    norm1_gain,
    norm2_gain,
    w_query,
    w_kv,
    w_out,
    w_gate,
    w_up,
    w_down,
    grad_output,
):
    row_count = lax.axis_size("row")
    full_rows = seq_ids.shape[0]
    slab_rows = full_rows // row_count
    slab_start = lax.axis_index("row") * slab_rows
    half_rows = tokens.shape[0]
    half_start = lax.axis_index("col") * half_rows
    head_width = w_kv.shape[1] // 2
    heads_local = w_query.shape[1] // head_width
    ff_local = w_gate.shape[1]
    score_scale = head_width ** (-0.5)
    w_both = jnp.concatenate([w_gate, w_up], axis=1)
    residual = tokens.astype(jnp.float32)
    factor_one, normed = norm_forward(residual, norm1_gain)
    gathered_in = gather_columns(normed)
    query_pre = spread_rows(gathered_in, w_query, 0)
    kv_pre = lax.psum(jnp.dot(gathered_in, w_kv, preferred_element_type=jnp.float32), "row")
    cosine_all, sine_all = rope_tables(positions, head_width)
    cosine_slab = lax.dynamic_slice_in_dim(cosine_all, slab_start, slab_rows, 0)[:, None, :]
    sine_slab = lax.dynamic_slice_in_dim(sine_all, slab_start, slab_rows, 0)[:, None, :]
    queries = rotate(
        query_pre.reshape(slab_rows, heads_local, head_width), cosine_slab, sine_slab
    ).astype(jnp.bfloat16)
    key_rows = rotate(kv_pre[:, :head_width], cosine_all, sine_all).astype(jnp.bfloat16)
    values = kv_pre[:, head_width:].astype(jnp.bfloat16)
    seq_slab = lax.dynamic_slice_in_dim(seq_ids, slab_start, slab_rows, 0)
    block_slab = lax.dynamic_slice_in_dim(block_ids, slab_start, slab_rows, 0)
    allowed = (seq_slab[:, None] == seq_ids[None, :]) & (block_ids[None, :] <= block_slab[:, None])
    head_queries = queries.transpose(1, 0, 2)

    def head_scores(query_head):
        scores = (
            lax.dot_general(query_head, key_rows, CONTRACT_LAST, preferred_element_type=jnp.float32)
            * score_scale
        )
        return jnp.where(allowed, scores, MASKED)

    def head_forward(query_head):
        scores = head_scores(query_head)
        row_max = jnp.max(scores, axis=1, keepdims=True)
        weights_exp = jnp.exp(scores - row_max)
        denominator = jnp.sum(weights_exp, axis=1, keepdims=True)
        probability = (weights_exp / denominator).astype(jnp.bfloat16)
        head_out = jnp.dot(probability, values, preferred_element_type=jnp.float32)
        return (head_out, (row_max + jnp.log(denominator))[:, 0])

    head_outs, log_totals = lax.map(head_forward, head_queries)
    attended = (
        head_outs.transpose(1, 0, 2)
        .reshape(slab_rows, heads_local * head_width)
        .astype(jnp.bfloat16)
    )
    out_product, _, kept_attended = fold_rows(attended, w_out, 0, None, True)
    hidden = residual + spread_columns(out_product)
    factor_two, normed_two = norm_forward(hidden, norm2_gain)
    gathered_mid = gather_columns(normed_two)
    both_proj = spread_rows(gathered_mid, w_both, 0)
    gate_proj = both_proj[:, :ff_local]
    up_proj = both_proj[:, ff_local:]
    sigmoid_gate = jax.nn.sigmoid(gate_proj)
    silu_gate = gate_proj * sigmoid_gate
    mixed_act = (silu_gate * up_proj).astype(jnp.bfloat16)
    down_product, _, kept_mixed = fold_rows(mixed_act, w_down, 0, None, True)
    output = hidden + spread_columns(down_product)
    down_grad = grad_output.astype(jnp.bfloat16)
    gathered_down = gather_columns(down_grad)
    mixed_grad = spread_rows(gathered_down, w_down, 1)
    grad_down_local = lax.dot_general(
        kept_mixed, gathered_down, CONTRACT_ROWS, preferred_element_type=jnp.float32
    )
    gate_grad = (
        mixed_grad * up_proj * sigmoid_gate * (1.0 + gate_proj * (1.0 - sigmoid_gate))
    ).astype(jnp.bfloat16)
    up_grad = (mixed_grad * silu_gate).astype(jnp.bfloat16)
    both_grad = jnp.concatenate([gate_grad, up_grad], axis=1)
    mid_product, grad_both_local, _ = fold_rows(both_grad, w_both, 1, gathered_mid, False)
    norm_two_part, gain_two_part = norm_backward(
        hidden, factor_two, norm2_gain, spread_columns(mid_product)
    )
    hidden_grad = grad_output + norm_two_part
    branch_grad = hidden_grad.astype(jnp.bfloat16)
    gathered_branch = gather_columns(branch_grad)
    attended_grad = spread_rows(gathered_branch, w_out, 1).astype(jnp.bfloat16)
    grad_out_local = lax.dot_general(
        kept_attended, gathered_branch, CONTRACT_ROWS, preferred_element_type=jnp.float32
    )
    head_grads = attended_grad.reshape(slab_rows, heads_local, head_width).transpose(1, 0, 2)

    def head_backward(running, head_inputs):
        key_acc, value_acc = running
        query_head, grad_head, log_total = head_inputs
        probs_full = jnp.exp(head_scores(query_head) - log_total[:, None])
        probs_low = probs_full.astype(jnp.bfloat16)
        value_acc = value_acc + lax.dot_general(
            probs_low, grad_head, CONTRACT_ROWS, preferred_element_type=jnp.float32
        )
        prob_grad = lax.dot_general(
            grad_head, values, CONTRACT_LAST, preferred_element_type=jnp.float32
        )
        row_dot = jnp.sum(probs_full * prob_grad, axis=1, keepdims=True)
        score_grad = (probs_full * (prob_grad - row_dot)).astype(jnp.bfloat16)
        query_grad = jnp.dot(score_grad, key_rows, preferred_element_type=jnp.float32) * score_scale
        key_acc = (
            key_acc
            + lax.dot_general(
                score_grad, query_head, CONTRACT_ROWS, preferred_element_type=jnp.float32
            )
            * score_scale
        )
        return ((key_acc, value_acc), query_grad)

    zero_rows = jnp.zeros((full_rows, head_width), jnp.float32)
    (key_acc, value_acc), query_grads = lax.scan(
        head_backward, (zero_rows, zero_rows), (head_queries, head_grads, log_totals)
    )
    key_total, value_total = (
        lax.psum(key_acc.astype(jnp.bfloat16), ("row", "col")).astype(jnp.float32),
        lax.psum(value_acc.astype(jnp.bfloat16), ("row", "col")).astype(jnp.float32),
    )
    query_pre_grad = (
        rotate_back(query_grads.transpose(1, 0, 2), cosine_slab, sine_slab)
        .reshape(slab_rows, heads_local * head_width)
        .astype(jnp.bfloat16)
    )
    kv_pre_grad = jnp.concatenate(
        [rotate_back(key_total, cosine_all, sine_all), value_total], axis=1
    ).astype(jnp.bfloat16)
    in_product, grad_query_local, _ = fold_rows(query_pre_grad, w_query, 1, gathered_in, False)
    kv_rows = lax.dynamic_slice_in_dim(kv_pre_grad, half_start, half_rows, 0)
    normed_grad = spread_columns(in_product) + lax.dot_general(
        kv_rows, w_kv, CONTRACT_LAST, preferred_element_type=jnp.float32
    )
    grad_kv_local = lax.dot_general(
        normed, kv_rows, CONTRACT_ROWS, preferred_element_type=jnp.float32
    )
    norm_one_part, gain_one_part = norm_backward(residual, factor_one, norm1_gain, normed_grad)
    input_grad = hidden_grad + norm_one_part
    reduced = (
        lax.psum_scatter(
            grad_query_local.astype(jnp.bfloat16), "dp", scatter_dimension=0, tiled=True
        ).astype(jnp.float32),
        lax.psum_scatter(
            grad_out_local.astype(jnp.bfloat16), "dp", scatter_dimension=0, tiled=True
        ).astype(jnp.float32),
        lax.psum_scatter(
            grad_both_local[:, :ff_local].astype(jnp.bfloat16),
            "dp",
            scatter_dimension=0,
            tiled=True,
        ).astype(jnp.float32),
        lax.psum_scatter(
            grad_both_local[:, ff_local:].astype(jnp.bfloat16),
            "dp",
            scatter_dimension=0,
            tiled=True,
        ).astype(jnp.float32),
        lax.psum_scatter(
            grad_down_local.astype(jnp.bfloat16), "dp", scatter_dimension=0, tiled=True
        ).astype(jnp.float32),
    )
    small_sums = (
        lax.psum_scatter(
            grad_kv_local.astype(jnp.bfloat16), ("dp", "col"), scatter_dimension=0, tiled=True
        ).astype(jnp.float32),
        lax.psum_scatter(
            jnp.stack([gain_one_part, gain_two_part], axis=1).astype(jnp.bfloat16),
            ("dp", "col"),
            scatter_dimension=0,
            tiled=True,
        ).astype(jnp.float32),
    )
    return (
        output,
        input_grad,
        reduced[0][None],
        small_sums[0][None],
        reduced[1][None],
        reduced[2][None],
        reduced[3][None],
        reduced[4][None],
        small_sums[1][:, 0][None, :],
        small_sums[1][:, 1][None, :],
    )


def solution(mesh):
    placed = (
        P(("dp", "col"), "row"),
        P("dp"),
        P("dp"),
        P("dp"),
        P("row"),
        P("row"),
        P("row", "col"),
        P("row", None),
        P("col", "row"),
        P("row", "col"),
        P("row", "col"),
        P("col", "row"),
        P(("dp", "col"), "row"),
    )
    return jax.shard_map(
        per_device,
        mesh=mesh,
        in_specs=placed,
        out_specs=(
            P(("dp", "col"), "row"),
            P(("dp", "col"), "row"),
            P("row", "dp", "col"),
            P("row", ("dp", "col"), None),
            P("col", "dp", "row"),
            P("row", "dp", "col"),
            P("row", "dp", "col"),
            P("col", "dp", "row"),
            P("row", ("dp", "col")),
            P("row", ("dp", "col")),
        ),
        check_vma=False,
    )
```

profile of v0, /device:TPU:0, one launch (start us, length us, event | category | flops | bytes accessed | tf_op | source)
XLA Modules:
  0.0 1890.7 jit_solution(8827306254039716388)
XLA Ops:
  8.9 8.4 psum.49
  21.1 33.5 %all-gather.9.cloned.1.call-done = bf16[2048,512]{1,0:T(8,128)(2,1)} async-done(((bf16[1024,512]{1,0:T(8,128)(2,1)}), bf16[2048,512]{1,0:T(8,128)(2,1)}) %all-gather.9.cloned.1.call-update) | async-done | bytes 2097168 | tf_op jit(solution)/shard_map/all_gather | solution.py:52
  58.3 7.5 fusion.66
  70.2 39.6 %all-reduce.4.cloned.1.call-done = f32[2048,256]{1,0:T(8,128)} async-done(((f32[2048,256]{1,0:T(8,128)}), f32[2048,256]{1,0:T(8,128)}) %all-reduce.4.cloned.1.call-update) | async-done | bytes 2097168 | tf_op jit(solution)/shard_map/psum | solution.py:139
  109.8 7.8 fusion.54
  122.4 62.0 %reduce-scatter.18.cloned.1.call-done = f32[512,1024]{1,0:T(8,128)} async-done(((f32[2048,1024]{1,0:T(8,128)}), f32[512,1024]{1,0:T(8,128)}) %reduce-scatter.18.cloned.1.call-update) | async-done | bytes 2097168 | tf_op jit(solution)/shard_map/reduce_scatter | solution.py:62
  192.5 66.3 %while.30 = (s32[]{:T(128)}, bf16[8,512,128]{1,2,0:T(8,128)(2,1)}, f32[8,512]{1,0:T(8,128)S(1)}, bf16[8,512,128]{2,1,0:T(8,128)(2,1)}, bf16[2048,128]{1,0:T(8,12...) while((s32[]{:T(128)}, bf16[8,512,128]{1,2,0:T(8,128)(2,1)}, ...), condition=%wide.region_7.8_spmd.clone.clone, body=%wide.region_4.7_spmd.clone.sunk.clone | while | flops 548404736 | bytes 30844036 | solution.py:169
  213.5 3.9 fusion.146
  258.9 34.6 %all-gather.11.cloned.1.call-done = bf16[2048,1024]{0,1:T(8,128)(2,1)} async-done(((bf16[512,1024]{0,1:T(8,128)(2,1)}), bf16[2048,1024]{0,1:T(8,128)(2,1)}) %all-gather.11.cloned.1.call-update) | async-done | bytes 4194320 | tf_op jit(solution)/shard_map/all_gather | solution.py:80
  293.5 6.2 convolution_convert_fusion.4
  302.7 29.0 %reduce-scatter.20.cloned.1.call-done = bf16[1024,512]{1,0:T(8,128)(2,1)} async-done(((bf16[2048,512]{1,0:T(8,128)(2,1)}), bf16[1024,512]{1,0:T(8,128)(2,1)}) %reduce-scatter.20.cloned.1.call-update) | async-done | bytes 1048592 | tf_op jit(solution)/shard_map/reduce_scatter | solution.py:56
  333.6 6.9 psum.51
  343.7 23.2 %all-gather.17.cloned.1.call-done = bf16[2048,512]{1,0:T(8,128)(2,1)} async-done(((bf16[1024,512]{1,0:T(8,128)(2,1)}), bf16[2048,512]{1,0:T(8,128)(2,1)}) %all-gather.17.cloned.1.call-update) | async-done | bytes 2097168 | tf_op jit(solution)/shard_map/all_gather | solution.py:52
  366.9 13.4 fusion.69
  386.0 16.3 all-gather.13.cloned.1.call-done
  402.2 34.2 %fusion.68 = f32[2048,5632]{1,0:T(8,128)} fusion(bf16[2048,512]{1,0:T(8,128)(2,1)} %all-gather.13.cloned.1.call-done, bf16[512,5632]{1,0:T(8,128)(2,1)} %constant_dynamic-update-slice_fusion.1), kind=kOutput, calls=%fused_computation.138 | convolution fusion | flops 11811160064 | bytes 54001664 | tf_op jit(solution)/shard_map/dot_general | solution.py:63
  436.6 135.3 %reduce-scatter.26.cloned.1.call-done = f32[512,2816]{1,0:T(8,128)} async-done(((f32[2048,2816]{1,0:T(8,128)}), f32[512,2816]{1,0:T(8,128)}) %reduce-scatter.26.cloned.1.call-update) | async-done | bytes 5767184 | tf_op jit(solution)/shard_map/reduce_scatter | solution.py:62
  571.8 318.6 %reduce-scatter.22.cloned.1.call-done = f32[512,5632]{1,0:T(8,128)} async-done(((f32[2048,5632]{1,0:T(8,128)}), f32[512,5632]{1,0:T(8,128)}) %reduce-scatter.22.cloned.1.call-update) | async-done | bytes 11534352 | tf_op jit(solution)/shard_map/reduce_scatter | solution.py:62
  890.4 8.8 multiply_convert_fusion.2
  902.3 143.1 %all-gather.19.cloned.1.call-done = bf16[2048,5632]{1,0:T(8,128)(2,1)} async-done(((bf16[512,5632]{1,0:T(8,128)(2,1)}), bf16[2048,5632]{1,0:T(8,128)(2,1)}) %all-gather.19.cloned.1.call-update) | async-done | bytes 23068688 | tf_op jit(solution)/shard_map/all_gather | solution.py:80
  1045.5 19.2 %convolution_convert_fusion.2 = bf16[2048,512]{1,0:T(8,128)(2,1)} fusion(bf16[2048,5632]{1,0:T(8,128)(2,1)} %all-gather.19.cloned.1.call-done, bf16[512,5632]{1,0:T(8,128)(2,1)} %constant_dynamic-update-slice_fusion.1), kind=kOutput, calls=%fused_computation.51 | convolution fusion | flops 11812208640 | bytes 30932992 | tf_op jit(solution)/shard_map/dot_general | solution.py:83
  1064.7 31.9 %reduce-scatter.28.cloned.1.call-done = bf16[1024,512]{1,0:T(8,128)(2,1)} async-done(((bf16[2048,512]{1,0:T(8,128)(2,1)}), bf16[1024,512]{1,0:T(8,128)(2,1)}) %reduce-scatter.28.cloned.1.call-update) | async-done | bytes 1048592 | tf_op jit(solution)/shard_map/reduce_scatter | solution.py:56
  1099.4 6.9 psum.52
  1110.1 32.3 %all-gather.21.cloned.1.call-done = bf16[2048,512]{1,0:T(8,128)(2,1)} async-done(((bf16[1024,512]{1,0:T(8,128)(2,1)}), bf16[2048,512]{1,0:T(8,128)(2,1)}) %all-gather.21.cloned.1.call-update) | async-done | bytes 2097168 | tf_op jit(solution)/shard_map/all_gather | solution.py:52
  1142.4 7.5 fusion.70
  1150.6 71.2 %reduce-scatter.30.cloned.1.call-done = f32[512,1024]{1,0:T(8,128)} async-done(((f32[2048,1024]{1,0:T(8,128)}), f32[512,1024]{1,0:T(8,128)}) %reduce-scatter.30.cloned.1.call-update) | async-done | bytes 2097168 | tf_op jit(solution)/shard_map/reduce_scatter | solution.py:62
  1224.6 133.2 %while.31 = (s32[]{:T(128)}, f32[2048,128]{1,0:T(8,128)}, f32[2048,128]{1,0:T(8,128)}, f32[8,512,128]{1,2,0:T(8,128)}, bf16[8,512,128]{2,1,0:T(8,128)(2,1)}, /*i...) while((s32[]{:T(128)}, f32[2048,128]{1,0:T(8,128)}, ...), condition=%wide.region_20.21_spmd.clone.clone, body=%wide.region_18.20_spmd.clone.sunk.clone | while | flops 1356135936 | bytes 87327544 | solution.py:235
  1234.4 4.0 fusion.157
  1364.3 11.0 convolution_convert_fusion.1
  1375.4 17.4 convolution_convert_fusion
  1396.6 6.2 convolution_convert_fusion.6
  1403.0 14.6 all-reduce.6.cloned.1.call-done
  1418.8 4.8 fusion.60
  1425.3 28.0 %all-gather.23.cloned.1.call-done = bf16[2048,1024]{0,1:T(8,128)(2,1)} async-done(((bf16[512,1024]{0,1:T(8,128)(2,1)}), bf16[2048,1024]{0,1:T(8,128)(2,1)}) %all-gather.23.cloned.1.call-update) | async-done | bytes 4194320 | tf_op jit(solution)/shard_map/all_gather | solution.py:80
  1453.3 6.2 convolution_convert_fusion.7
  1459.5 6.7 convolution_convert_fusion.3
  1466.3 9.9 convolution_convert_fusion.5
  1476.2 35.5 %reduce-scatter.44.cloned.1.call-done = bf16[704,512]{1,0:T(8,128)(2,1)} async-done(((bf16[2816,512]{1,0:T(8,128)(2,1)}), bf16[704,512]{1,0:T(8,128)(2,1)}) %reduce-scatter.44.cloned.1.call-update) | async-done | bytes 720912 | tf_op jit(solution)/shard_map/reduce_scatter | solution.py:279
  1514.2 55.9 %reduce-scatter.42.cloned.1.call-done = bf16[128,2816]{1,0:T(8,128)(2,1)} async-done(((bf16[512,2816]{1,0:T(8,128)(2,1)}), bf16[128,2816]{1,0:T(8,128)(2,1)}) %reduce-scatter.42.cloned.1.call-update) | async-done | bytes 720912 | tf_op jit(solution)/shard_map/reduce_scatter | solution.py:273
  1572.4 56.2 %reduce-scatter.40.cloned.1.call-done = bf16[128,2816]{1,0:T(8,128)(2,1)} async-done(((bf16[512,2816]{1,0:T(8,128)(2,1)}), bf16[128,2816]{1,0:T(8,128)(2,1)}) %reduce-scatter.40.cloned.1.call-update) | async-done | bytes 720912 | tf_op jit(solution)/shard_map/reduce_scatter | solution.py:267
  1630.8 27.0 %reduce-scatter.38.cloned.1.call-done = bf16[256,512]{1,0:T(8,128)(2,1)} async-done(((bf16[1024,512]{1,0:T(8,128)(2,1)}), bf16[256,512]{1,0:T(8,128)(2,1)}) %reduce-scatter.38.cloned.1.call-update) | async-done | bytes 262160 | tf_op jit(solution)/shard_map/reduce_scatter | solution.py:264
  1659.6 62.0 %reduce-scatter.36.cloned.1.call-done = bf16[64,256]{1,0:T(8,128)(2,1)} async-done(((bf16[512,256]{1,0:T(8,128)(2,1)}), bf16[64,256]{1,0:T(8,128)(2,1)}) %reduce-scatter.36.cloned.1.call-update) | async-done | bytes 32784 | tf_op jit(solution)/shard_map/reduce_scatter | solution.py:284
  1723.0 27.1 %reduce-scatter.34.cloned.1.call-done = bf16[128,1024]{1,0:T(8,128)(2,1)} async-done(((bf16[512,1024]{1,0:T(8,128)(2,1)}), bf16[128,1024]{1,0:T(8,128)(2,1)}) %reduce-scatter.34.cloned.1.call-update) | async-done | bytes 262160 | tf_op jit(solution)/shard_map/reduce_scatter | solution.py:261
  1751.9 31.6 %reduce-scatter.32.cloned.1.call-done = bf16[1024,512]{1,0:T(8,128)(2,1)} async-done(((bf16[2048,512]{1,0:T(8,128)(2,1)}), bf16[1024,512]{1,0:T(8,128)(2,1)}) %reduce-scatter.32.cloned.1.call-update) | async-done | bytes 1048592 | tf_op jit(solution)/shard_map/reduce_scatter | solution.py:56
  1788.1 6.8 psum.55
  1795.0 23.1 %reduce-scatter.24.cloned.1.call-done = bf16[1024,512]{1,0:T(8,128)(2,1)} async-done(((bf16[2048,512]{1,0:T(8,128)(2,1)}), bf16[1024,512]{1,0:T(8,128)(2,1)}) %reduce-scatter.24.cloned.1.call-update) | async-done | bytes 1048592 | tf_op jit(solution)/shard_map/reduce_scatter | solution.py:56
  1818.0 5.4 fusion.41
  1823.5 59.1 %reduce-scatter.46.cloned.1.call-done = bf16[64,2]{1,0:T(8,128)(2,1)} async-done(((bf16[512,2]{1,0:T(8,128)(2,1)}), bf16[64,2]{1,0:T(8,128)(2,1)}) %reduce-scatter.46.cloned.1.call-update) | async-done | bytes 272
  (373 shorter events, 275.6 us)
Async XLA Ops:
  7.2 359.7 %copy-start = (bf16[2816,512]{1,0:T(8,128)(2,1)S(1)}, bf16[2816,512]{1,0:T(8,128)(2,1)}, u32[]{:S(2)}) copy-start(bf16[2816,512]{1,0:T(8,128)(2,1)} %param.28) | copy-start | bytes 8650756
  7.2 47.4 %copy-start.15 = (bf16[512,256]{1,0:T(8,128)(2,1)S(1)}, bf16[512,256]{1,0:T(8,128)(2,1)}, u32[]{:S(2)}) copy-start(bf16[512,256]{1,0:T(8,128)(2,1)} %param.24) | copy-start | bytes 786436
  7.2 47.4 %all-gather.9.cloned.1.call-start = ((), (), s32[]{:S(2)}) async-start(), calls=%async_computation.15 | async-start | bytes 3145728 | tf_op jit(solution)/shard_map/all_gather | solution.py:52
  21.0 88.8 %all-reduce.4.cloned.1.call-start = ((), (), s32[]{:S(2)}) async-start(), calls=%async_computation.17 | async-start | bytes 4194304 | tf_op jit(solution)/shard_map/psum | solution.py:139
  58.2 126.1 %reduce-scatter.18.cloned.1.call-start = ((), (), s32[]{:S(2)}) async-start(), calls=%async_computation.16 | async-start | bytes 10485760 | tf_op jit(solution)/shard_map/reduce_scatter | solution.py:62
  65.8 227.7 %all-gather.11.cloned.1.call-start = ((), (), s32[]{:S(2)}) async-start(), calls=%async_computation.18 | async-start | bytes 5242880 | tf_op jit(solution)/shard_map/all_gather | solution.py:80
  66.5 51.1 %copy-start.16 = (f32[2048]{0:T(1024)}, f32[2048]{0:T(1024)S(1)}, u32[]{:S(2)}) copy-start(f32[2048]{0:T(1024)S(1)} %convert_element_type.116) | copy-start | bytes 24580
  69.1 48.4 %copy-start.26 = (f32[64]{0:T(128)}, f32[64]{0:T(128)S(1)}, u32[]{:S(2)}) copy-start(f32[64]{0:T(128)S(1)} %multiply_power_fusion) | copy-start | bytes 772
  117.7 69.5 %copy-start.11 = (f32[512,64]{0,1:T(8,128)}, f32[512,64]{0,1:T(8,128)S(1)}, u32[]{:S(2)}) copy-start(f32[512,64]{0,1:T(8,128)S(1)} %copy.36) | copy-start | bytes 393220
  258.8 72.8 %reduce-scatter.20.cloned.1.call-start = ((), (), s32[]{:S(2)}) async-start(), calls=%async_computation.19 | async-start | bytes 3145728 | tf_op jit(solution)/shard_map/reduce_scatter | solution.py:56
  299.7 67.2 %all-gather.17.cloned.1.call-start = ((), (), s32[]{:S(2)}) async-start(), calls=%async_computation.24 | async-start | bytes 3145728 | tf_op jit(solution)/shard_map/all_gather | solution.py:52
  302.4 38.1 %copy-start.20 = (f32[512]{0:T(512)S(1)}, f32[512]{0:T(512)}, u32[]{:S(2)}) copy-start(f32[512]{0:T(512)} %param.22) | copy-start | bytes 6148
  302.5 99.8 %all-gather.13.cloned.1.call-start = ((), (), s32[]{:S(2)}) async-start(), calls=%async_computation.20 | async-start | bytes 3145728 | tf_op jit(solution)/shard_map/all_gather | solution.py:52
  343.6 228.2 %reduce-scatter.26.cloned.1.call-start = ((), (), s32[]{:S(2)}) async-start(), calls=%async_computation.25 | async-start | bytes 28835840 | tf_op jit(solution)/shard_map/reduce_scatter | solution.py:62
  380.3 510.1 %reduce-scatter.22.cloned.1.call-start = ((), (), s32[]{:S(2)}) async-start(), calls=%async_computation.21 | async-start | bytes 57671680 | tf_op jit(solution)/shard_map/reduce_scatter | solution.py:62
  380.4 3.8 copy-start.10
  436.5 608.9 %all-gather.19.cloned.1.call-start = ((), (), s32[]{:S(2)}) async-start(), calls=%async_computation.26 | async-start | bytes 28835840 | tf_op jit(solution)/shard_map/all_gather | solution.py:80
  902.1 194.5 %reduce-scatter.28.cloned.1.call-start = ((), (), s32[]{:S(2)}) async-start(), calls=%async_computation.27 | async-start | bytes 3145728 | tf_op jit(solution)/shard_map/reduce_scatter | solution.py:56
  1064.6 77.8 %all-gather.21.cloned.1.call-start = ((), (), s32[]{:S(2)}) async-start(), calls=%async_computation.28 | async-start | bytes 3145728 | tf_op jit(solution)/shard_map/all_gather | solution.py:52
  1110.1 111.8 %reduce-scatter.30.cloned.1.call-start = ((), (), s32[]{:S(2)}) async-start(), calls=%async_computation.29 | async-start | bytes 10485760 | tf_op jit(solution)/shard_map/reduce_scatter | solution.py:62
  1150.0 214.3 %all-gather.15.cloned.1.call-start = ((), (), s32[]{:S(2)}) async-start(), calls=%async_computation.22 | async-start | bytes 14417920 | tf_op jit(solution)/shard_map/all_gather | solution.py:80
  1150.6 267.1 %all-reduce.6.cloned.1.call-start = ((), (), s32[]{:S(2)}) async-start(), calls=%async_computation.39 | async-start | bytes 2097152 | tf_op jit(solution)/shard_map/psum | solution.py:239
  1234.4 4.7 copy-start.3
  1251.5 3.9 copy-start.3
  1268.2 3.8 copy-start.3
  1284.7 3.8 copy-start.3
  1301.3 3.8 copy-start.3
  1317.8 3.8 copy-start.3
  1334.4 3.8 copy-start.3
  1350.9 3.8 copy-start.3
  1357.8 3.5 copy-start.13
  1360.8 92.4 %all-gather.23.cloned.1.call-start = ((), (), s32[]{:S(2)}) async-start(), calls=%async_computation.30 | async-start | bytes 5242880 | tf_op jit(solution)/shard_map/all_gather | solution.py:80
  1364.3 147.5 %reduce-scatter.44.cloned.1.call-start = ((), (), s32[]{:S(2)}) async-start(), calls=%async_computation.37 | async-start | bytes 3604480 | tf_op jit(solution)/shard_map/reduce_scatter | solution.py:279
  1375.4 194.7 %reduce-scatter.42.cloned.1.call-start = ((), (), s32[]{:S(2)}) async-start(), calls=%async_computation.36 | async-start | bytes 3604480 | tf_op jit(solution)/shard_map/reduce_scatter | solution.py:273
  1395.8 232.8 %reduce-scatter.40.cloned.1.call-start = ((), (), s32[]{:S(2)}) async-start(), calls=%async_computation.35 | async-start | bytes 3604480 | tf_op jit(solution)/shard_map/reduce_scatter | solution.py:267
  1396.5 261.3 %reduce-scatter.38.cloned.1.call-start = ((), (), s32[]{:S(2)}) async-start(), calls=%async_computation.34 | async-start | bytes 1310720 | tf_op jit(solution)/shard_map/reduce_scatter | solution.py:264
  1402.8 16.1 copy-start.17
  1402.8 16.1 copy-start.27
  1402.8 318.8 %reduce-scatter.36.cloned.1.call-start = ((), (), s32[]{:S(2)}) async-start(), calls=%async_computation.33 | async-start | bytes 294912 | tf_op jit(solution)/shard_map/reduce_scatter | solution.py:284
  1417.6 6.1 copy-start.14
  1418.8 5.1 copy-start.9
  1425.2 324.9 %reduce-scatter.34.cloned.1.call-start = ((), (), s32[]{:S(2)}) async-start(), calls=%async_computation.32 | async-start | bytes 1310720 | tf_op jit(solution)/shard_map/reduce_scatter | solution.py:261
  1459.5 324.0 %reduce-scatter.32.cloned.1.call-start = ((), (), s32[]{:S(2)}) async-start(), calls=%async_computation.31 | async-start | bytes 3145728 | tf_op jit(solution)/shard_map/reduce_scatter | solution.py:56
  1466.2 351.8 %reduce-scatter.24.cloned.1.call-start = ((), (), s32[]{:S(2)}) async-start(), calls=%async_computation.23 | async-start | bytes 3145728 | tf_op jit(solution)/shard_map/reduce_scatter | solution.py:56
  1476.2 406.5 %reduce-scatter.46.cloned.1.call-start = ((), (), s32[]{:S(2)}) async-start(), calls=%async_computation.38 | async-start | bytes 147456
  1572.4 211.1 %copy-start.19 = (f32[1024]{0:T(1024)S(1)}, f32[1024]{0:T(1024)}, u32[]{:S(2)}) copy-start(f32[1024]{0:T(1024)} %copy-done.18) | copy-start | bytes 12292
  1572.4 211.1 %copy-start.22 = (f32[512]{0:T(512)S(1)}, f32[512]{0:T(512)}, u32[]{:S(2)}) copy-start(f32[512]{0:T(512)} %param.21) | copy-start | bytes 6148
  1751.9 66.2 %copy-start.21 = (f32[1024]{0:T(1024)S(1)}, f32[1024]{0:T(1024)}, u32[]{:S(2)}) copy-start(f32[1024]{0:T(1024)} %get-tuple-element.300) | copy-start | bytes 12292
  (56 other events, 116.5 us)
Sparse Core Ops, SparseCore 0:
  21.1 33.3 all-gather.8
  58.4 51.3 all-reduce.3
  112.5 71.7 reduce-scatter.17
  259.0 34.4 all-gather.10
  299.8 31.8 reduce-scatter.19
  333.7 33.1 all-gather.16
  369.1 33.1 all-gather.12
  405.0 166.7 reduce-scatter.25
  574.4 315.9 reduce-scatter.21
  902.2 143.2 all-gather.18
  1064.8 31.8 reduce-scatter.27
  1110.2 32.2 all-gather.20
  1150.1 71.7 reduce-scatter.29
  1223.4 76.1 all-gather.14
  1361.0 56.6 all-reduce.5
  1419.7 33.5 all-gather.22
  1455.5 56.1 reduce-scatter.43
  1514.0 56.0 reduce-scatter.41
  1572.5 56.0 reduce-scatter.39
  1630.8 26.9 reduce-scatter.37
  1661.7 59.8 reduce-scatter.35
  1723.9 26.1 reduce-scatter.33
  1753.0 30.4 reduce-scatter.31
  1786.2 31.8 reduce-scatter.23
  1821.7 60.8 reduce-scatter.45
where the time goes:
time: 1900 us; the launch traced here: 1890 us
  waiting for transfers between devices  1390 us (73%)
  matrix products  303 us (16%)
  other arithmetic  86.5 us (5%)
  local copies, waits for them, and re-layouts  63 us (3%)
  blocking collectives  28.9 us (2%)
    reduce_scatter x4, waiting for transfers between devices, spread_rows(): lax.psum_scatter(lax.dot_general(gathered, matrix, (((1,), (contract_dim,...  587 us
    all_gather x4, waiting for transfers between devices, fold_rows(): shard_rows = lax.all_gather(operand, 'row', axis=0, tiled=True)  206 us
    reduce_scatter x4, waiting for transfers between devices, spread_columns(): lax.psum_scatter(operand.astype(jnp.bfloat16), 'col', scatter_dimension=0...  116 us
    all_gather x4, waiting for transfers between devices, gather_columns(): return lax.all_gather(operand, 'col', axis=0, tiled=True)  105 us
    dot_general x4, matrix products, spread_rows(): lax.dot_general(gathered, matrix, (((1,), (contract_dim,)), ((), ())), pr...  62.7 us
    reduce_scatter x1, waiting for transfers between devices, per_device(): lax.psum_scatter(grad_kv_local.astype(jnp.bfloat16), ('dp', 'col'), scatt...  62 us
    unnamed x26, waiting for transfers between devices  60.7 us
    reduce_scatter x1, waiting for transfers between devices, per_device(): lax.psum_scatter(grad_both_local[:, :ff_local].astype(jnp.bfloat16), 'dp'...  56.2 us
  transfers between devices with their start and end apart: 25, of which 24 were waited for; matrix products, arithmetic and copies ran while one was open for 15% of the time, Pallas kernels for 0%

commit v1 on v0

--- a/solution.py
+++ b/solution.py
@@ -9,6 +9,27 @@
 MASKED = -1e30
 CONTRACT_ROWS = (((0,), (0,)), ((), ()))
 CONTRACT_LAST = (((1,), (1,)), ((), ()))
+
+
+def ring_gather(x, axis, dim):
+    length, index, extent = (lax.axis_size(axis), lax.axis_index(axis), x.shape[dim])
+    right = [(i, (i + 1) % length) for i in range(length)]
+    backward = [(i, (i - 1) % length) for i in range(length)]
+    filled = jnp.zeros((*x.shape[:dim], length * extent, *x.shape[dim + 1 :]), x.dtype)
+    filled = lax.dynamic_update_slice_in_dim(filled, x, index * extent, axis=dim)
+    from_left = from_right = x
+    half = length // 2
+    for lap in range(1, half + 1):
+        from_left = lax.ppermute(from_left, axis, right)
+        filled = lax.dynamic_update_slice_in_dim(
+            filled, from_left, (index - lap) % length * extent, axis=dim
+        )
+        if lap < length - half:
+            from_right = lax.ppermute(from_right, axis, backward)
+            filled = lax.dynamic_update_slice_in_dim(
+                filled, from_right, (index + lap) % length * extent, axis=dim
+            )
+    return filled
 
 
 def rope_tables(positions, head_width):
@@ -77,7 +98,7 @@
     grad_shape = (partner.shape[1], operand.shape[1]) if partner is not None else (1, 1)
     grad_zero = jnp.zeros(grad_shape, jnp.float32)
     kept_zero = jnp.zeros((full_rows, operand.shape[1]) if keeping else (1, 1), operand.dtype)
-    shard_rows = lax.all_gather(operand, "row", axis=0, tiled=True)
+    shard_rows = ring_gather(operand, "row", 0)
     grad_acc = grad_zero
     kept_rows = kept_zero
     row_block = lax.dot_general(

time: 1900 us -> 2030 us (1.068)
  local copies, waits for them, and re-layouts: 63 us -> 120 us
  waiting for transfers between devices: 1390 us -> 1440 us
    ppermute x0 -> x12, waiting for transfers between devices: none -> 359 us  [the longest x8 359 us: ring_gather(): from_left = lax.ppermute(from_left, axis, right)]
    all_gather x4 -> x0, waiting for transfers between devices: 206 us -> none  [fold_rows(): shard_rows = lax.all_gather(operand, 'row', axis=0, tiled=True)]
    reduce_scatter x4, waiting for transfers between devices: 587 us -> 515 us  [spread_rows(): lax.psum_scatter(lax.dot_general(gathered, matrix, (((1,), (contract_dim,...]
    dynamic_update_slice x0 -> x14, local copies, waits for them, and re-layouts: none -> 33.1 us  [the longest x8 20.5 us: ring_gather(): lax.dynamic_update_slice_in_dim(filled, from_left, (index - lap) % length...]
    reduce_scatter x1, waiting for transfers between devices: 35.5 us -> 9.72 us  [per_device(): lax.psum_scatter(grad_down_local.astype(jnp.bfloat16), 'dp', scatter_dime...]
    unnamed x26 -> x22, waiting for transfers between devices: 60.7 us -> 59.6 us
  transfers between devices with their start and end apart: 25 -> 33, of which waited for: 24 -> 28; matrix products, arithmetic and copies ran while one was open for 15% -> 11% of each run, Pallas kernels for 0% -> 0%
where the time goes in v1:
time: 2030 us; the launch traced here: 2020 us
  waiting for transfers between devices  1440 us (71%)
  matrix products  299 us (15%)
  local copies, waits for them, and re-layouts  120 us (6%)
  other arithmetic  103 us (5%)
  blocking collectives  28.9 us (1%)
    reduce_scatter x4, waiting for transfers between devices, spread_rows(): lax.psum_scatter(lax.dot_general(gathered, matrix, (((1,), (contract_dim,...  515 us
    ppermute x8, waiting for transfers between devices, ring_gather(): from_left = lax.ppermute(from_left, axis, right)  359 us
    reduce_scatter x4, waiting for transfers between devices, spread_columns(): lax.psum_scatter(operand.astype(jnp.bfloat16), 'col', scatter_dimension=0...  115 us
    all_gather x4, waiting for transfers between devices, gather_columns(): return lax.all_gather(operand, 'col', axis=0, tiled=True)  105 us
    dot_general x4, matrix products, spread_rows(): lax.dot_general(gathered, matrix, (((1,), (contract_dim,)), ((), ())), pr...  62.7 us
    reduce_scatter x1, waiting for transfers between devices, per_device(): lax.psum_scatter(grad_kv_local.astype(jnp.bfloat16), ('dp', 'col'), scatt...  61.9 us
    unnamed x22, waiting for transfers between devices  59.6 us
    reduce_scatter x1, waiting for transfers between devices, per_device(): lax.psum_scatter(grad_both_local[:, :ff_local].astype(jnp.bfloat16), 'dp'...  56 us
  transfers between devices with their start and end apart: 33, of which 28 were waited for; matrix products, arithmetic and copies ran while one was open for 11% of the time, Pallas kernels for 0%

profile of v1, /device:TPU:0, one launch (start us, length us, event | category | flops | bytes accessed | tf_op | source)
XLA Modules:
  0.0 2020.8 jit_solution(3905626334866049143)
XLA Ops:
  8.9 8.4 psum.49
  21.1 33.5 %all-gather.5.cloned.1.call-done = bf16[2048,512]{1,0:T(8,128)(2,1)} async-done(((bf16[1024,512]{1,0:T(8,128)(2,1)}), bf16[2048,512]{1,0:T(8,128)(2,1)}) %all-gather.5.cloned.1.call-update) | async-done | bytes 2097168 | tf_op jit(solution)/shard_map/all_gather | solution.py:73
  58.3 7.5 fusion.66
  70.2 39.6 %all-reduce.4.cloned.1.call-done = f32[2048,256]{1,0:T(8,128)} async-done(((f32[2048,256]{1,0:T(8,128)}), f32[2048,256]{1,0:T(8,128)}) %all-reduce.4.cloned.1.call-update) | async-done | bytes 2097168 | tf_op jit(solution)/shard_map/psum | solution.py:160
  109.8 7.8 fusion.54
  122.4 62.0 %reduce-scatter.18.cloned.1.call-done = f32[512,1024]{1,0:T(8,128)} async-done(((f32[2048,1024]{1,0:T(8,128)}), f32[512,1024]{1,0:T(8,128)}) %reduce-scatter.18.cloned.1.call-update) | async-done | bytes 2097168 | tf_op jit(solution)/shard_map/reduce_scatter | solution.py:83
  192.5 72.4 %while.30 = (s32[]{:T(128)}, bf16[8,512,128]{1,2,0:T(8,128)(2,1)}, f32[8,512]{1,0:T(8,128)S(1)}, bf16[8,512,128]{2,1,0:T(8,128)(2,1)}, bf16[2048,128]{1,0:T(8,12...) while((s32[]{:T(128)}, bf16[8,512,128]{1,2,0:T(8,128)(2,1)}, ...), condition=%wide.region_7.8_spmd.clone.clone, body=%wide.region_4.7_spmd.clone.sunk.clone | while | flops 548404736 | bytes 30844036 | solution.py:190
  266.6 23.5 %collective-permute-done = bf16[512,1024]{0,1:T(8,128)(2,1)} collective-permute-done((bf16[512,1024]{0,1:T(8,128)(2,1)}, bf16[512,1024]{0,1:T(8,128)(2,1)}, u32[]{:S(2)}, u32[]{:S(2)}) %collective-permute-start) | collective-permute-done | bytes 1048608 | tf_op jit(solution)/shard_map/ppermute | solution.py:23
  294.6 10.2 collective-permute-done.2
  314.8 28.9 %reduce-scatter.20.cloned.1.call-done = bf16[1024,512]{1,0:T(8,128)(2,1)} async-done(((bf16[2048,512]{1,0:T(8,128)(2,1)}), bf16[1024,512]{1,0:T(8,128)(2,1)}) %reduce-scatter.20.cloned.1.call-update) | async-done | bytes 1048592 | tf_op jit(solution)/shard_map/reduce_scatter | solution.py:77
  345.7 6.9 psum.51
  355.8 23.1 %all-gather.9.cloned.1.call-done = bf16[2048,512]{1,0:T(8,128)(2,1)} async-done(((bf16[1024,512]{1,0:T(8,128)(2,1)}), bf16[2048,512]{1,0:T(8,128)(2,1)}) %all-gather.9.cloned.1.call-update) | async-done | bytes 2097168 | tf_op jit(solution)/shard_map/all_gather | solution.py:73
  378.9 13.4 fusion.69
  398.0 16.1 all-gather.7.cloned.1.call-done
  414.1 34.3 %fusion.68 = f32[2048,5632]{1,0:T(8,128)} fusion(bf16[2048,512]{1,0:T(8,128)(2,1)} %all-gather.7.cloned.1.call-done, bf16[512,5632]{1,0:T(8,128)(2,1)} %constant_dynamic-update-slice_fusion.1), kind=kOutput, calls=%fused_computation.154 | convolution fusion | flops 11811160064 | bytes 54001664 | tf_op jit(solution)/shard_map/dot_general | solution.py:84
  448.9 134.9 %reduce-scatter.26.cloned.1.call-done = f32[512,2816]{1,0:T(8,128)} async-done(((f32[2048,2816]{1,0:T(8,128)}), f32[512,2816]{1,0:T(8,128)}) %reduce-scatter.26.cloned.1.call-update) | async-done | bytes 5767184 | tf_op jit(solution)/shard_map/reduce_scatter | solution.py:83
  583.7 318.6 %reduce-scatter.22.cloned.1.call-done = f32[512,5632]{1,0:T(8,128)} async-done(((f32[2048,5632]{1,0:T(8,128)}), f32[512,5632]{1,0:T(8,128)}) %reduce-scatter.22.cloned.1.call-update) | async-done | bytes 11534352 | tf_op jit(solution)/shard_map/reduce_scatter | solution.py:83
  902.3 9.0 multiply_convert_fusion.2
  911.3 8.0 broadcast_in_dim.86
  919.3 7.7 pad_maximum_fusion
  928.7 124.4 %collective-permute-done.6 = bf16[512,5632]{1,0:T(8,128)(2,1)S(1)} collective-permute-done((bf16[512,5632]{1,0:T(8,128)(2,1)}, bf16[512,5632]{1,0:T(8,128)(2,1)S(1)}, u32[]{:S(2)}, u32[]{:S(2)}) %collective-permute-start.6) | collective-permute-done | bytes 5767200 | tf_op jit(solution)/shard_map/ppermute | solution.py:23
  1058.9 59.0 %collective-permute-done.8 = bf16[512,5632]{1,0:T(8,128)(2,1)S(1)} collective-permute-done((bf16[512,5632]{1,0:T(8,128)(2,1)S(1)}, bf16[512,5632]{1,0:T(8,128)(2,1)S(1)}, u32[]{:S(2)}, u32[]{:S(2)}) %collective-permute-start.8) | collective-permute-done | bytes 5767200 | tf_op jit(solution)/shard_map/ppermute | solution.py:23
  1120.7 19.2 convolution_convert_fusion.2
  1139.9 31.7 %reduce-scatter.28.cloned.1.call-done = bf16[1024,512]{1,0:T(8,128)(2,1)} async-done(((bf16[2048,512]{1,0:T(8,128)(2,1)}), bf16[1024,512]{1,0:T(8,128)(2,1)}) %reduce-scatter.28.cloned.1.call-update) | async-done | bytes 1048592 | tf_op jit(solution)/shard_map/reduce_scatter | solution.py:77
  1175.0 6.8 psum.52
  1185.7 32.3 %all-gather.11.cloned.1.call-done = bf16[2048,512]{1,0:T(8,128)(2,1)} async-done(((bf16[1024,512]{1,0:T(8,128)(2,1)}), bf16[2048,512]{1,0:T(8,128)(2,1)}) %all-gather.11.cloned.1.call-update) | async-done | bytes 2097168 | tf_op jit(solution)/shard_map/all_gather | solution.py:73
  1218.0 7.5 fusion.70
  1230.7 9.7 constant_dynamic-update-slice_fusion.14
  1242.1 106.4 %collective-permute-done.3 = bf16[512,2816]{1,0:T(8,128)(2,1)} collective-permute-done((bf16[512,2816]{1,0:T(8,128)(2,1)}, bf16[512,2816]{1,0:T(8,128)(2,1)}, u32[]{:S(2)}, u32[]{:S(2)}) %collective-permute-start.3) | collective-permute-done | bytes 2883616 | tf_op jit(solution)/shard_map/ppermute | solution.py:23
  1356.0 26.7 %collective-permute-done.5 = bf16[512,2816]{1,0:T(8,128)(2,1)} collective-permute-done((bf16[512,2816]{1,0:T(8,128)(2,1)}, bf16[512,2816]{1,0:T(8,128)(2,1)}, u32[]{:S(2)}, u32[]{:S(2)}) %collective-permute-start.5) | collective-permute-done | bytes 2883616 | tf_op jit(solution)/shard_map/ppermute | solution.py:23
  1389.0 131.3 %while.31 = (s32[]{:T(128)}, f32[2048,128]{1,0:T(8,128)}, f32[2048,128]{1,0:T(8,128)}, f32[8,512,128]{1,2,0:T(8,128)}, bf16[8,512,128]{2,1,0:T(8,128)(2,1)}, /*i...) while((s32[]{:T(128)}, f32[2048,128]{1,0:T(8,128)}, ...), condition=%wide.region_20.21_spmd.clone.clone, body=%wide.region_18.20_spmd.clone.sunk.clone | while | flops 1356135936 | bytes 87327544 | solution.py:256
  1524.6 10.8 convolution_convert_fusion.1
  1535.7 17.5 convolution_convert_fusion
  1556.7 6.3 convolution_convert_fusion.6
  1572.7 10.3 all-reduce.6.cloned.1.call-done
  1584.2 8.9 collective-permute-done.9
  1615.7 6.2 convolution_convert_fusion.3
  1622.0 10.0 convolution_convert_fusion.5
  1632.0 9.7 reduce-scatter.44.cloned.1.call-done
  1644.2 55.9 %reduce-scatter.42.cloned.1.call-done = bf16[128,2816]{1,0:T(8,128)(2,1)} async-done(((bf16[512,2816]{1,0:T(8,128)(2,1)}), bf16[128,2816]{1,0:T(8,128)(2,1)}) %reduce-scatter.42.cloned.1.call-update) | async-done | bytes 720912 | tf_op jit(solution)/shard_map/reduce_scatter | solution.py:294
  1702.4 56.0 %reduce-scatter.40.cloned.1.call-done = bf16[128,2816]{1,0:T(8,128)(2,1)} async-done(((bf16[512,2816]{1,0:T(8,128)(2,1)}), bf16[128,2816]{1,0:T(8,128)(2,1)}) %reduce-scatter.40.cloned.1.call-update) | async-done | bytes 720912 | tf_op jit(solution)/shard_map/reduce_scatter | solution.py:288
  1760.7 27.0 %reduce-scatter.38.cloned.1.call-done = bf16[256,512]{1,0:T(8,128)(2,1)} async-done(((bf16[1024,512]{1,0:T(8,128)(2,1)}), bf16[256,512]{1,0:T(8,128)(2,1)}) %reduce-scatter.38.cloned.1.call-update) | async-done | bytes 262160 | tf_op jit(solution)/shard_map/reduce_scatter | solution.py:285
  1789.5 61.9 %reduce-scatter.36.cloned.1.call-done = bf16[64,256]{1,0:T(8,128)(2,1)} async-done(((bf16[512,256]{1,0:T(8,128)(2,1)}), bf16[64,256]{1,0:T(8,128)(2,1)}) %reduce-scatter.36.cloned.1.call-update) | async-done | bytes 32784 | tf_op jit(solution)/shard_map/reduce_scatter | solution.py:305
  1852.7 27.0 %reduce-scatter.34.cloned.1.call-done = bf16[128,1024]{1,0:T(8,128)(2,1)} async-done(((bf16[512,1024]{1,0:T(8,128)(2,1)}), bf16[128,1024]{1,0:T(8,128)(2,1)}) %reduce-scatter.34.cloned.1.call-update) | async-done | bytes 262160 | tf_op jit(solution)/shard_map/reduce_scatter | solution.py:282
  1881.5 31.6 %reduce-scatter.32.cloned.1.call-done = bf16[1024,512]{1,0:T(8,128)(2,1)} async-done(((bf16[2048,512]{1,0:T(8,128)(2,1)}), bf16[1024,512]{1,0:T(8,128)(2,1)}) %reduce-scatter.32.cloned.1.call-update) | async-done | bytes 1048592 | tf_op jit(solution)/shard_map/reduce_scatter | solution.py:77
  1917.7 6.9 psum.55
  1924.6 23.0 %reduce-scatter.24.cloned.1.call-done = bf16[1024,512]{1,0:T(8,128)(2,1)} async-done(((bf16[2048,512]{1,0:T(8,128)(2,1)}), bf16[1024,512]{1,0:T(8,128)(2,1)}) %reduce-scatter.24.cloned.1.call-update) | async-done | bytes 1048592 | tf_op jit(solution)/shard_map/reduce_scatter | solution.py:77
  1953.5 58.7 %reduce-scatter.46.cloned.1.call-done = bf16[64,2]{1,0:T(8,128)(2,1)} async-done(((bf16[512,2]{1,0:T(8,128)(2,1)}), bf16[64,2]{1,0:T(8,128)(2,1)}) %reduce-scatter.46.cloned.1.call-update) | async-done | bytes 272
  (426 shorter events, 360.1 us)
Async XLA Ops:
  7.2 371.7 %copy-start = (bf16[2816,512]{1,0:T(8,128)(2,1)S(1)}, bf16[2816,512]{1,0:T(8,128)(2,1)}, u32[]{:S(2)}) copy-start(bf16[2816,512]{1,0:T(8,128)(2,1)} %param.28) | copy-start | bytes 8650756
  7.2 47.4 %copy-start.17 = (bf16[512,256]{1,0:T(8,128)(2,1)S(1)}, bf16[512,256]{1,0:T(8,128)(2,1)}, u32[]{:S(2)}) copy-start(bf16[512,256]{1,0:T(8,128)(2,1)} %param.24) | copy-start | bytes 786436
  7.2 47.4 %all-gather.5.cloned.1.call-start = ((), (), s32[]{:S(2)}) async-start(), calls=%async_computation.15 | async-start | bytes 3145728 | tf_op jit(solution)/shard_map/all_gather | solution.py:73
  21.0 88.7 %all-reduce.4.cloned.1.call-start = ((), (), s32[]{:S(2)}) async-start(), calls=%async_computation.17 | async-start | bytes 4194304 | tf_op jit(solution)/shard_map/psum | solution.py:160
  58.2 126.1 %reduce-scatter.18.cloned.1.call-start = ((), (), s32[]{:S(2)}) async-start(), calls=%async_computation.16 | async-start | bytes 10485760 | tf_op jit(solution)/shard_map/reduce_scatter | solution.py:83
  65.8 277.9 %reduce-scatter.20.cloned.1.call-start = ((), (), s32[]{:S(2)}) async-start(), calls=%async_computation.18 | async-start | bytes 3145728 | tf_op jit(solution)/shard_map/reduce_scatter | solution.py:77
  66.5 51.1 %copy-start.20 = (f32[2048]{0:T(1024)}, f32[2048]{0:T(1024)S(1)}, u32[]{:S(2)}) copy-start(f32[2048]{0:T(1024)S(1)} %convert_element_type.116) | copy-start | bytes 24580
  69.1 48.4 %copy-start.36 = (f32[64]{0:T(128)}, f32[64]{0:T(128)S(1)}, u32[]{:S(2)}) copy-start(f32[64]{0:T(128)S(1)} %multiply_power_fusion) | copy-start | bytes 772
  117.7 69.5 %copy-start.13 = (f32[512,64]{0,1:T(8,128)}, f32[512,64]{0,1:T(8,128)S(1)}, u32[]{:S(2)}) copy-start(f32[512,64]{0,1:T(8,128)S(1)} %copy.36) | copy-start | bytes 393220
  264.9 25.2 %collective-permute-start = (bf16[512,1024]{0,1:T(8,128)(2,1)}, bf16[512,1024]{0,1:T(8,128)(2,1)}, u32[]{:S(2)}, u32[]{:S(2)}) collective-permute-start(bf16[512,1024]{0,1:T(8,128)(2,1)} %bitcast.150), channel_id=1, source_target_pairs={{0,2},{2,4},{4,6},{6,0},{1,3},{3,5},{5,7},{7,1},{8,10},{10,12},{12... | collective-permute-start | bytes 3145736 | tf_op jit(solution)/shard_map/ppermute | solution.py:23
  264.9 28.4 %collective-permute-start.1 = (bf16[512,1024]{0,1:T(8,128)(2,1)}, bf16[512,1024]{0,1:T(8,128)(2,1)}, u32[]{:S(2)}, u32[]{:S(2)}) collective-permute-start(bf16[512,1024]{0,1:T(8,128)(2,1)} %bitcast.151), channel_id=1, source_target_pairs={{0,6},{2,0},{4,2},{6,4},{1,7},{3,1},{5,3},{7,5},{8,14},{10,8},{12,... | collective-permute-start | bytes 3145736 | tf_op jit(solution)/shard_map/ppermute | solution.py:28
  290.1 14.7 collective-permute-start.2
  312.0 40.6 %copy-start.28 = (f32[512]{0:T(512)S(1)}, f32[512]{0:T(512)}, u32[]{:S(2)}) copy-start(f32[512]{0:T(512)} %param.22) | copy-start | bytes 6148
  312.0 66.9 %all-gather.9.cloned.1.call-start = ((), (), s32[]{:S(2)}) async-start(), calls=%async_computation.22 | async-start | bytes 3145728 | tf_op jit(solution)/shard_map/all_gather | solution.py:73
  314.8 99.3 %all-gather.7.cloned.1.call-start = ((), (), s32[]{:S(2)}) async-start(), calls=%async_computation.19 | async-start | bytes 3145728 | tf_op jit(solution)/shard_map/all_gather | solution.py:73
  352.6 829.2 %copy-start.18 = (f32[1024]{0:T(1024)}, f32[1024]{0:T(1024)S(1)}, u32[]{:S(2)}) copy-start(f32[1024]{0:T(1024)S(1)} %get-tuple-element.306) | copy-start | bytes 12292
  352.6 829.2 %copy-start.24 = (f32[1024]{0:T(1024)}, f32[1024]{0:T(1024)S(1)}, u32[]{:S(2)}) copy-start(f32[1024]{0:T(1024)S(1)} %get-tuple-element.305) | copy-start | bytes 12292
  355.7 228.0 %reduce-scatter.26.cloned.1.call-start = ((), (), s32[]{:S(2)}) async-start(), calls=%async_computation.23 | async-start | bytes 28835840 | tf_op jit(solution)/shard_map/reduce_scatter | solution.py:83
  392.4 509.9 %reduce-scatter.22.cloned.1.call-start = ((), (), s32[]{:S(2)}) async-start(), calls=%async_computation.20 | async-start | bytes 57671680 | tf_op jit(solution)/shard_map/reduce_scatter | solution.py:83
  448.4 723.2 %reduce-scatter.28.cloned.1.call-start = ((), (), s32[]{:S(2)}) async-start(), calls=%async_computation.24 | async-start | bytes 3145728 | tf_op jit(solution)/shard_map/reduce_scatter | solution.py:77
  927.0 126.1 %collective-permute-start.6 = (bf16[512,5632]{1,0:T(8,128)(2,1)}, bf16[512,5632]{1,0:T(8,128)(2,1)S(1)}, u32[]{:S(2)}, u32[]{:S(2)}) collective-permute-start(bf16[512,5632]{1,0:T(8,128)(2,1)} %get-tuple-element.289), channel_id=1, source_target_pairs={{0,2},{2,4},{4,6},{6,0},{1,3},{3,5},{5,7},{7,1},{8,10},{10,12},{12... | collective-permute-start | bytes 17301512 | tf_op jit(solution)/shard_map/ppermute | solution.py:23
  927.0 129.0 %collective-permute-start.7 = (bf16[512,5632]{1,0:T(8,128)(2,1)}, bf16[512,5632]{1,0:T(8,128)(2,1)S(1)}, u32[]{:S(2)}, u32[]{:S(2)}) collective-permute-start(bf16[512,5632]{1,0:T(8,128)(2,1)} %get-tuple-element.289), channel_id=1, source_target_pairs={{0,6},{2,0},{4,2},{6,4},{1,7},{3,1},{5,3},{7,5},{8,14},{10,8},{12,... | collective-permute-start | bytes 17301512 | tf_op jit(solution)/shard_map/ppermute | solution.py:28
  1053.1 64.8 %collective-permute-start.8 = (bf16[512,5632]{1,0:T(8,128)(2,1)S(1)}, bf16[512,5632]{1,0:T(8,128)(2,1)S(1)}, u32[]{:S(2)}, u32[]{:S(2)}) collective-permute-start(bf16[512,5632]{1,0:T(8,128)(2,1)S(1)} %collective-permute-done.6), channel_id=1, source_target_pairs={{0,2},{2,4},{4,6},{6,0},{1,3},{3,5},{5,7},{7,1},{8,10},{10,12},{12... | collective-permute-start | bytes 17301512 | tf_op jit(solution)/shard_map/ppermute | solution.py:23
  1139.9 78.1 %all-gather.11.cloned.1.call-start = ((), (), s32[]{:S(2)}) async-start(), calls=%async_computation.25 | async-start | bytes 3145728 | tf_op jit(solution)/shard_map/all_gather | solution.py:73
  1185.6 200.7 %reduce-scatter.30.cloned.1.call-start = ((), (), s32[]{:S(2)}) async-start(), calls=%async_computation.26 | async-start | bytes 10485760 | tf_op jit(solution)/shard_map/reduce_scatter | solution.py:83
  1225.6 357.4 %all-reduce.6.cloned.1.call-start = ((), (), s32[]{:S(2)}) async-start(), calls=%async_computation.35 | async-start | bytes 2097152 | tf_op jit(solution)/shard_map/psum | solution.py:260
  1240.4 108.1 %collective-permute-start.3 = (bf16[512,2816]{1,0:T(8,128)(2,1)}, bf16[512,2816]{1,0:T(8,128)(2,1)}, u32[]{:S(2)}, u32[]{:S(2)}) collective-permute-start(bf16[512,2816]{1,0:T(8,128)(2,1)} %get-tuple-element.280), channel_id=1, source_target_pairs={{0,2},{2,4},{4,6},{6,0},{1,3},{3,5},{5,7},{7,1},{8,10},{10,12},{12... | collective-permute-start | bytes 8650760 | tf_op jit(solution)/shard_map/ppermute | solution.py:23
  1240.4 112.0 %collective-permute-start.4 = (bf16[512,2816]{1,0:T(8,128)(2,1)}, bf16[512,2816]{1,0:T(8,128)(2,1)}, u32[]{:S(2)}, u32[]{:S(2)}) collective-permute-start(bf16[512,2816]{1,0:T(8,128)(2,1)} %get-tuple-element.280), channel_id=1, source_target_pairs={{0,6},{2,0},{4,2},{6,4},{1,7},{3,1},{5,3},{7,5},{8,14},{10,8},{12,... | collective-permute-start | bytes 8650760 | tf_op jit(solution)/shard_map/ppermute | solution.py:28
  1348.5 34.2 %collective-permute-start.5 = (bf16[512,2816]{1,0:T(8,128)(2,1)}, bf16[512,2816]{1,0:T(8,128)(2,1)}, u32[]{:S(2)}, u32[]{:S(2)}) collective-permute-start(bf16[512,2816]{1,0:T(8,128)(2,1)} %collective-permute-done.3), channel_id=1, source_target_pairs={{0,2},{2,4},{4,6},{6,0},{1,3},{3,5},{5,7},{7,1},{8,10},{10,12},{12... | collective-permute-start | bytes 8650760 | tf_op jit(solution)/shard_map/ppermute | solution.py:23
  1524.5 117.2 %reduce-scatter.44.cloned.1.call-start = ((), (), s32[]{:S(2)}) async-start(), calls=%async_computation.33 | async-start | bytes 3604480 | tf_op jit(solution)/shard_map/reduce_scatter | solution.py:300
  1535.4 164.6 %reduce-scatter.42.cloned.1.call-start = ((), (), s32[]{:S(2)}) async-start(), calls=%async_computation.32 | async-start | bytes 3604480 | tf_op jit(solution)/shard_map/reduce_scatter | solution.py:294
  1556.1 202.3 %reduce-scatter.40.cloned.1.call-start = ((), (), s32[]{:S(2)}) async-start(), calls=%async_computation.31 | async-start | bytes 3604480 | tf_op jit(solution)/shard_map/reduce_scatter | solution.py:288
  1556.7 231.0 %reduce-scatter.38.cloned.1.call-start = ((), (), s32[]{:S(2)}) async-start(), calls=%async_computation.30 | async-start | bytes 1310720 | tf_op jit(solution)/shard_map/reduce_scatter | solution.py:285
  1563.1 288.2 %reduce-scatter.36.cloned.1.call-start = ((), (), s32[]{:S(2)}) async-start(), calls=%async_computation.29 | async-start | bytes 294912 | tf_op jit(solution)/shard_map/reduce_scatter | solution.py:305
  1566.1 27.0 %collective-permute-start.9 = (bf16[512,1024]{0,1:T(8,128)(2,1)}, bf16[512,1024]{0,1:T(8,128)(2,1)}, u32[]{:S(2)}, u32[]{:S(2)}) collective-permute-start(bf16[512,1024]{0,1:T(8,128)(2,1)} %bitcast.6), channel_id=1, source_target_pairs={{0,2},{2,4},{4,6},{6,0},{1,3},{3,5},{5,7},{7,1},{8,10},{10,12},{12... | collective-permute-start | bytes 3145736 | tf_op jit(solution)/shard_map/ppermute | solution.py:23
  1566.4 38.9 %collective-permute-start.10 = (bf16[512,1024]{0,1:T(8,128)(2,1)}, bf16[512,1024]{0,1:T(8,128)(2,1)}, u32[]{:S(2)}, u32[]{:S(2)}) collective-permute-start(bf16[512,1024]{0,1:T(8,128)(2,1)} %bitcast.6), channel_id=1, source_target_pairs={{0,6},{2,0},{4,2},{6,4},{1,7},{3,1},{5,3},{7,5},{8,14},{10,8},{12,... | collective-permute-start | bytes 3145736 | tf_op jit(solution)/shard_map/ppermute | solution.py:28
  1593.1 14.5 collective-permute-start.11
  1602.5 277.2 %reduce-scatter.34.cloned.1.call-start = ((), (), s32[]{:S(2)}) async-start(), calls=%async_computation.28 | async-start | bytes 1310720 | tf_op jit(solution)/shard_map/reduce_scatter | solution.py:282
  1615.7 297.5 %reduce-scatter.32.cloned.1.call-start = ((), (), s32[]{:S(2)}) async-start(), calls=%async_computation.27 | async-start | bytes 3145728 | tf_op jit(solution)/shard_map/reduce_scatter | solution.py:77
  1621.9 325.7 %reduce-scatter.24.cloned.1.call-start = ((), (), s32[]{:S(2)}) async-start(), calls=%async_computation.21 | async-start | bytes 3145728 | tf_op jit(solution)/shard_map/reduce_scatter | solution.py:77
  1632.0 380.2 %reduce-scatter.46.cloned.1.call-start = ((), (), s32[]{:S(2)}) async-start(), calls=%async_computation.34 | async-start | bytes 147456
  1644.2 269.0 %copy-start.23 = (f32[1024]{0:T(1024)S(1)}, f32[1024]{0:T(1024)}, u32[]{:S(2)}) copy-start(f32[1024]{0:T(1024)} %copy-done.22) | copy-start | bytes 12292
  1644.2 269.0 %copy-start.32 = (f32[512]{0:T(512)S(1)}, f32[512]{0:T(512)}, u32[]{:S(2)}) copy-start(f32[512]{0:T(512)} %param.21) | copy-start | bytes 6148
  1881.5 66.1 %copy-start.19 = (f32[1024]{0:T(1024)S(1)}, f32[1024]{0:T(1024)}, u32[]{:S(2)}) copy-start(f32[1024]{0:T(1024)} %copy-done.18) | copy-start | bytes 12292
  1881.5 66.1 %copy-start.25 = (f32[1024]{0:T(1024)S(1)}, f32[1024]{0:T(1024)}, u32[]{:S(2)}) copy-start(f32[1024]{0:T(1024)} %copy-done.24) | copy-start | bytes 12292
  1881.5 66.1 %copy-start.27 = (f32[1024]{0:T(1024)S(1)}, f32[1024]{0:T(1024)}, u32[]{:S(2)}) copy-start(f32[1024]{0:T(1024)} %copy-done.26) | copy-start | bytes 12292
  1881.5 66.1 %copy-start.29 = (f32[512]{0:T(512)S(1)}, f32[512]{0:T(512)}, u32[]{:S(2)}) copy-start(f32[512]{0:T(512)} %param.22) | copy-start | bytes 6148
  1881.5 66.1 %copy-start.30 = (f32[1024]{0:T(1024)S(1)}, f32[1024]{0:T(1024)}, u32[]{:S(2)}) copy-start(f32[1024]{0:T(1024)} %get-tuple-element.303) | copy-start | bytes 12292
  (75 other events, 310.4 us)
Sparse Core Ops, SparseCore 0:
  21.1 33.3 all-gather.4
  58.3 51.3 all-reduce.3
  112.5 71.7 reduce-scatter.17
  312.1 31.5 reduce-scatter.19
  345.8 33.1 all-gather.8
  381.0 33.1 all-gather.6
  416.9 166.7 reduce-scatter.25
  586.3 315.9 reduce-scatter.21
  1140.0 31.5 reduce-scatter.27
  1185.7 32.2 all-gather.10
  1225.7 119.0 reduce-scatter.29
  1524.6 58.2 all-reduce.5
  1585.4 56.3 reduce-scatter.43
  1644.0 56.0 reduce-scatter.41
  1702.3 56.0 reduce-scatter.39
  1760.7 26.9 reduce-scatter.37
  1791.4 59.8 reduce-scatter.35
  1853.5 26.1 reduce-scatter.33
  1882.6 30.4 reduce-scatter.31
  1915.8 31.8 reduce-scatter.23
  1951.3 60.8 reduce-scatter.45
